TPU v7x, 32 devices: a whole 2x2x4 slice. The times are simulated.
32 devices in a mesh: occ: 8 (over z, y), vir: 4 (over x, core).
Axes of the slice: x: 2, y: 2, z: 4, core: 2. Of those that a mesh axis runs over, the one named last changes fastest.
Arguments:
- amplitudes: bfloat16 [16384, 8192], P('occ', 'vir'), may hold values from -6 to 6
- integrals: bfloat16 [8192, 8192], P('occ', 'vir'), may hold values from -0.0625 to 0.0625
- other_terms: bfloat16 [16384, 8192], P('occ', 'vir'), may hold values from -6 to 6
- occ_irrep: int32 [4], replicated, may hold values from 0 to 3, as said below
- vir_irrep: int32 [32], replicated, may hold values from 0 to 3
- pair_tiles: int32 [8, 2], replicated, may hold values from 0 to 31
- spin_mask: int32 [16, 8], replicated, may hold values 0 or 1
- occ_energy: float32 [128], replicated, may hold values from -2 to -0.5
- vir_energy: float32 [1024], replicated, may hold values from 0.2 to 3
Outputs:
- updated: bfloat16 [16384, 8192], P('occ', 'vir')
Inputs may be any that keep to these rules, and one draw needn't show every extreme that they name: `occ_irrep`: the labels are not all equal. `pair_tiles`: tiles of one pair may repeat across pairs.
All inputs are finite; a program needn't handle non-finite values.
Results may differ from a plain program's by a relative error of at most 0.001.
Values may be sent and summed in bfloat16 or wider, within the bound.
A program may use at most 448 MiB of HBM per device.

v0:
```python
import jax
import jax.numpy as jnp
from jax import lax
from jax.sharding import PartitionSpec as P

TILE = 32
OTILES = 4


def lookup(index, table):
    hits = index[:, None] == jnp.arange(table.shape[0], dtype=jnp.int32)[None, :]
    return jnp.sum(
        jnp.where(hits[:, :, None], table[None, :, :], jnp.zeros_like(table)[None, :, :]), axis=1
    )


def symmetry(occ_irrep, vir_irrep, pair_tiles, spin_mask):
    first = lookup(pair_tiles[:, 0], vir_irrep[:, None])[:, 0]
    second = lookup(pair_tiles[:, 1], vir_irrep[:, None])[:, 0]
    pair_irrep = jnp.bitwise_xor(first, second)
    occ_pair = jnp.bitwise_xor(occ_irrep[:, None], occ_irrep[None, :]).reshape(-1)
    allowed = jnp.where(
        (occ_pair[:, None] == pair_irrep[None, :]) & (spin_mask == 1), 1.0, 0.0
    ).astype(jnp.float32)
    coupled = jnp.where(pair_irrep[:, None] == pair_irrep[None, :], 1.0, 0.0).astype(jnp.float32)
    return (allowed, coupled)


def add_block(amp_cols, slab_rows):
    return jnp.dot(amp_cols, slab_rows, preferred_element_type=jnp.float32)


def per_device(
    amplitudes,
    integrals,
    other_terms,
    occ_irrep,
    vir_irrep,
    pair_tiles,
    spin_mask,
    occ_energy,
    vir_energy,
):
    square = TILE * TILE
    allowed, coupled = symmetry(occ_irrep, vir_irrep, pair_tiles, spin_mask)
    height = amplitudes.shape[0]
    width = amplitudes.shape[1]
    slab_height = integrals.shape[0]
    row_global = lax.axis_index("occ") * height + jnp.arange(height, dtype=jnp.int32)
    col_global = lax.axis_index("vir") * width + jnp.arange(width, dtype=jnp.int32)
    row_block = row_global // square
    col_pair = col_global // square
    row_allowed = lookup(row_block, allowed)
    amp_keep = lookup(col_pair, row_allowed.T).T
    masked_amp = jnp.where(amp_keep > 0.5, amplitudes, jnp.zeros_like(amplitudes))
    slab_pair = (
        lax.axis_index("occ") * slab_height + jnp.arange(slab_height, dtype=jnp.int32)
    ) // square
    int_keep = lookup(col_pair, lookup(slab_pair, coupled).T).T
    masked_slab = jnp.where(int_keep > 0.5, integrals, jnp.zeros_like(integrals))
    whole_amp = lax.all_gather(masked_amp, "vir", axis=1, tiled=True)
    ladder = add_block(whole_amp, lax.all_gather(masked_slab, "occ", axis=0, tiled=True))
    inner = row_global % square
    occ_first = row_block // OTILES * TILE + inner // TILE
    occ_second = row_block % OTILES * TILE + inner % TILE
    occ_sum = (
        lookup(occ_first, occ_energy[:, None])[:, 0] + lookup(occ_second, occ_energy[:, None])[:, 0]
    )
    col_inner = col_global % square
    tile_first = lookup(col_pair, pair_tiles[:, 0:1])[:, 0]
    tile_second = lookup(col_pair, pair_tiles[:, 1:2])[:, 0]
    vir_first = tile_first * TILE + col_inner // TILE
    vir_second = tile_second * TILE + col_inner % TILE
    vir_sum = (
        lookup(vir_first, vir_energy[:, None])[:, 0] + lookup(vir_second, vir_energy[:, None])[:, 0]
    )
    denom = occ_sum[:, None] - vir_sum[None, :]
    updated = amp_keep * ((ladder + other_terms.astype(jnp.float32)) / denom)
    return updated.astype(jnp.bfloat16)


def solution(mesh):
    in_specs = (P("occ", "vir"), P("occ", "vir"), P("occ", "vir"), P(), P(), P(), P(), P(), P())
    out_specs = P("occ", "vir")
    return jax.shard_map(
        per_device, mesh=mesh, in_specs=in_specs, out_specs=out_specs, check_vma=False
    )
```

profile of v0, /device:TPU:20, one launch (start us, length us, event | category | flops | bytes accessed | tf_op | source)
XLA Modules:
  0.0 1028.9 jit_solution(16806289375461734369)
XLA Ops:
  6.5 0.0 all-gather.3.cloned.1.call-start
  6.6 0.8 slice_bitcast_fusion.1
  7.3 0.8 broadcast_xor_fusion
  8.1 0.1 xor.34
  8.2 0.9 select_reduce_fusion.10
  9.1 0.8 and_select_fusion
  9.8 0.1 copy.11
  10.0 0.3 iota_compare_fusion.4
  10.3 0.2 select_reduce_fusion.6
  10.5 54.9 %select_reduce_fusion = f32[2048,2048]{1,0:T(8,128)} fusion(f32[8,2048]{1,0:T(8,128)S(1)} %bitcast.17, pred[2048,8]{1,0:T(8,128)(4,1)S(1)} %iota_compare_fusion.4), kind=kLoop, calls=%fused_computation | loop fusion | flops 62914560 | bytes 16859136 | tf_op jit(solution)/shard_map/reduce_sum | solution.py:12
  65.4 17.6 %copy.12 = f32[2048,2048]{0,1:T(8,128)} copy(f32[2048,2048]{1,0:T(8,128)} %select_reduce_fusion) | data formatting | bytes 33554432 | tf_op jit(solution)/shard_map/reduce_sum | solution.py:12
  83.0 12.2 %fusion.1 = bf16[2048,2048]{1,0:T(8,128)(2,1)} fusion(bf16[2048,2048]{1,0:T(8,128)(2,1)} %param.9, f32[2048,2048]{0,1:T(8,128)} %copy.12), kind=kLoop, calls=%fused_computation.5 | loop fusion | flops 8388608 | bytes 33554432 | tf_op jit(solution)/shard_map/jit(_where)/select_n | solution.py:55
  95.3 0.0 all-gather.3.cloned.1.call-update
  95.3 0.2 all-gather.5.cloned.1.call-start
  95.5 6.4 copy.13
  101.9 0.1 compare_select_fusion
  102.0 0.1 select_reduce_fusion.7
  102.1 24.7 %select_reduce_fusion.1 = f32[2048,1024]{1,0:T(8,128)} fusion(f32[8,1024]{1,0:T(8,128)S(1)} %bitcast.18, pred[2048,8]{1,0:T(8,128)(4,1)S(1)} %iota_compare_fusion.4), kind=kLoop, calls=%fused_computation.1 | loop fusion | flops 31457280 | bytes 8437760 | tf_op jit(solution)/shard_map/reduce_sum | solution.py:12
  126.8 0.0 copy-start.1
  126.8 0.0 copy-start
  126.8 7.6 bitcast_select_fusion
  134.4 0.0 all-gather.5.cloned.1.call-update
  134.4 0.1 select_reduce_fusion.8
  134.6 0.0 copy-done.1
  134.6 2.8 select_reduce_fusion.2
  137.5 0.0 copy-done
  137.5 1.3 select_reduce_fusion.4
  138.8 159.2 %all-gather.3.cloned.1.call-done = bf16[2048,8192]{1,0:T(8,128)(2,1)} async-done(((bf16[2048,2048]{1,0:T(8,128)(2,1)}), bf16[2048,8192]{1,0:T(8,128)(2,1)}) %all-gather.3.cloned.1.call-update) | async-done | bytes 33554448 | tf_op jit(solution)/shard_map/all_gather | solution.py:61
  298.0 638.4 %all-gather.5.cloned.1.call-done = bf16[8192,2048]{0,1:T(8,128)(2,1)} async-done(((bf16[1024,2048]{0,1:T(8,128)(2,1)}), bf16[8192,2048]{0,1:T(8,128)(2,1)}) %all-gather.5.cloned.1.call-update) | async-done | bytes 33554448 | tf_op jit(solution)/shard_map/all_gather | solution.py:62
  936.4 85.7 %fusion = bf16[2048,2048]{1,0:T(8,128)(2,1)} fusion(f32[2048,2048]{0,1:T(8,128)} %copy.12, bf16[2048,2048]{1,0:T(8,128)(2,1)} %param.11, f32[2048]{0:T(1024)S(1)} %add.188, f32[2048]{0:T(1024)S(1)} %add.183, bf16[2048,8192]{1,0:T(8,128)(2,1)} %all-gather.3.cloned.1.call-done, bf16[8192,2048]{0,1:T(8,128)(2,1)} %all-gather.5.cloned.1.call-done), kind=kOutput, calls=%fused_computation.4 | convolution fusion | flops 68744642560 | bytes 100679680 | tf_op jit(solution)/shard_map/dot_general | solution.py:30
  (10 shorter events, 0.1 us)
Async XLA Ops:
  6.5 291.5 %all-gather.3.cloned.1.call-start = ((), (), s32[]{:S(2)}) async-start(), calls=%async_computation | async-start | bytes 41943040 | tf_op jit(solution)/shard_map/all_gather | solution.py:61
  95.3 841.1 %all-gather.5.cloned.1.call-start = ((), (), s32[]{:S(2)}) async-start(), calls=%async_computation.1 | async-start | bytes 37748736 | tf_op jit(solution)/shard_map/all_gather | solution.py:62
  126.8 7.8 copy-start.1
  126.8 10.6 %copy-start = (f32[128]{0:T(128)S(1)}, f32[128]{0:T(128)}, u32[]{:S(2)}) copy-start(f32[128]{0:T(128)} %param.16) | copy-start | bytes 1540
Sparse Core Ops, SparseCore 0:
  95.4 202.5 all-gather.2
  299.5 636.8 all-gather.4
where the time goes:
time: 1030 us
  waiting for transfers between devices  798 us (77%)
  other arithmetic  107 us (10%)
  matrix products  85.7 us (8%)
  local copies, waits for them, and re-layouts  24.9 us (2%)
  between operations  13.5 us (1%)
    all_gather x1, waiting for transfers between devices, per_device(): lax.all_gather(masked_slab, 'occ', axis=0, tiled=True)  638 us
    all_gather x1, waiting for transfers between devices, per_device(): whole_amp = lax.all_gather(masked_amp, 'vir', axis=1, tiled=True)  159 us
    dot_general x1, matrix products, add_block(): return jnp.dot(amp_cols, slab_rows, preferred_element_type=jnp.float32)  85.7 us
    reduce_sum x8, other arithmetic, lookup(): jnp.sum(jnp.where(hits[:, :, None], table[None, :, :], jnp.zeros_like(tab...  85 us
  transfers between devices with their start and end apart: 2, of which 2 were waited for; matrix products, arithmetic and copies ran while one was open for 4% of the time, Pallas kernels for 0%

commit v1 on v0

--- a/solution.py
+++ b/solution.py
@@ -1,10 +1,17 @@
+import functools
+
 import jax
 import jax.numpy as jnp
 from jax import lax
+from jax.experimental import pallas as pl
+from jax.experimental.pallas import tpu as pltpu
 from jax.sharding import PartitionSpec as P
 
 TILE = 32
 OTILES = 4
+SQUARE = TILE * TILE
+PIECES = 4
+STEP_COLS = 256
 
 
 def lookup(index, table):
@@ -26,11 +33,7 @@
     return (allowed, coupled)
 
 
-def add_block(amp_cols, slab_rows):
-    return jnp.dot(amp_cols, slab_rows, preferred_element_type=jnp.float32)
-
-
-def per_device(
+def dense_device(
     amplitudes,
     integrals,
     other_terms,
@@ -41,32 +44,32 @@
     occ_energy,
     vir_energy,
 ):
-    square = TILE * TILE
     allowed, coupled = symmetry(occ_irrep, vir_irrep, pair_tiles, spin_mask)
     height = amplitudes.shape[0]
     width = amplitudes.shape[1]
     slab_height = integrals.shape[0]
     row_global = lax.axis_index("occ") * height + jnp.arange(height, dtype=jnp.int32)
     col_global = lax.axis_index("vir") * width + jnp.arange(width, dtype=jnp.int32)
-    row_block = row_global // square
-    col_pair = col_global // square
+    row_block = row_global // SQUARE
+    col_pair = col_global // SQUARE
     row_allowed = lookup(row_block, allowed)
     amp_keep = lookup(col_pair, row_allowed.T).T
     masked_amp = jnp.where(amp_keep > 0.5, amplitudes, jnp.zeros_like(amplitudes))
     slab_pair = (
         lax.axis_index("occ") * slab_height + jnp.arange(slab_height, dtype=jnp.int32)
-    ) // square
+    ) // SQUARE
     int_keep = lookup(col_pair, lookup(slab_pair, coupled).T).T
     masked_slab = jnp.where(int_keep > 0.5, integrals, jnp.zeros_like(integrals))
     whole_amp = lax.all_gather(masked_amp, "vir", axis=1, tiled=True)
-    ladder = add_block(whole_amp, lax.all_gather(masked_slab, "occ", axis=0, tiled=True))
-    inner = row_global % square
+    whole_slab = lax.all_gather(masked_slab, "occ", axis=0, tiled=True)
+    ladder = jnp.dot(whole_amp, whole_slab, preferred_element_type=jnp.float32)
+    inner = row_global % SQUARE
     occ_first = row_block // OTILES * TILE + inner // TILE
     occ_second = row_block % OTILES * TILE + inner % TILE
     occ_sum = (
         lookup(occ_first, occ_energy[:, None])[:, 0] + lookup(occ_second, occ_energy[:, None])[:, 0]
     )
-    col_inner = col_global % square
+    col_inner = col_global % SQUARE
     tile_first = lookup(col_pair, pair_tiles[:, 0:1])[:, 0]
     tile_second = lookup(col_pair, pair_tiles[:, 1:2])[:, 0]
     vir_first = tile_first * TILE + col_inner // TILE
@@ -79,6 +82,300 @@
     return updated.astype(jnp.bfloat16)
 
 
+def pack_kernel(index_ref, block_ref, slot_ref):
+    slot_ref[0] = block_ref[...]
+
+
+def pack(index, array, slots):
+    half = SQUARE // 2
+    return pl.pallas_call(
+        pack_kernel,
+        out_shape=jax.ShapeDtypeStruct((slots, SQUARE, SQUARE), array.dtype),
+        grid_spec=pltpu.PrefetchScalarGridSpec(
+            num_scalar_prefetch=1,
+            grid=(slots, 2),
+            in_specs=[
+                pl.BlockSpec((half, SQUARE), lambda j, r, ix: (ix[j] // 2 * 2 + r, ix[j] % 2))
+            ],
+            out_specs=pl.BlockSpec((1, half, SQUARE), lambda j, r, ix: (j, r, 0)),
+        ),
+        name="pack",
+    )(index, array)
+
+
+def exchange_kernel(
+    n, cap_a, cap_b, a_ref, b_ref, ag_ref, bg_ref, own_sem, a_send, a_recv, b_send, b_recv
+):
+    o = lax.axis_index("occ")
+    v = lax.axis_index("vir")
+
+    def place(pos):
+        late = pos // (n // 2)
+        return 2 * pos * (1 - late) + (2 * (n - 1 - pos) + 1) * late
+
+    odd = o % 2
+    pos = (o // 2) * (1 - odd) + (n - 1 - o // 2) * odd
+    right = place((pos + 1) % n)
+    left = place((pos + n - 1) % n)
+    mate = v + 1 - 2 * (v % 2)
+    across = (v + 2) % 4
+    mesh_id = pl.DeviceIdType.MESH
+
+    barrier = pltpu.get_barrier_semaphore()
+    for target in ((right, v), (left, v), (o, mate), (o, across)):
+        pl.semaphore_signal(barrier, inc=1, device_id=target, device_id_type=mesh_id)
+    pl.semaphore_wait(barrier, 4)
+
+    def a_copy(which, src, owner, target):
+        return pltpu.make_async_remote_copy(
+            src_ref=src,
+            dst_ref=ag_ref.at[owner, pl.ds(0, cap_a)],
+            send_sem=a_send.at[which],
+            recv_sem=a_recv.at[which],
+            device_id=(o, target),
+            device_id_type=mesh_id,
+        )
+
+    rows = SQUARE // PIECES
+
+    def b_copy(step, piece):
+        cut = pl.ds(piece * rows, rows)
+        if piece < PIECES // 2:
+            owner, target = place((pos + n - step) % n), right
+        else:
+            owner, target = place((pos + step) % n), left
+        src = b_ref.at[:, cut] if step == 0 else bg_ref.at[owner, pl.ds(0, cap_b), cut]
+        return pltpu.make_async_remote_copy(
+            src_ref=src,
+            dst_ref=bg_ref.at[owner, pl.ds(0, cap_b), cut],
+            send_sem=b_send.at[step, piece],
+            recv_sem=b_recv.at[step, piece],
+            device_id=(target, v),
+            device_id_type=mesh_id,
+        )
+
+    order = [p for pair in zip(range(PIECES // 2), range(PIECES // 2, PIECES)) for p in pair]
+    b_copies = {}
+    for piece in order:
+        b_copies[0, piece] = b_copy(0, piece)
+        b_copies[0, piece].start()
+    to_across = a_copy(0, a_ref, v, across)
+    to_across.start()
+    to_mate = a_copy(1, a_ref, v, mate)
+    to_mate.start()
+    own_b = pltpu.make_async_copy(b_ref, bg_ref.at[o, pl.ds(0, cap_b)], own_sem.at[0])
+    own_b.start()
+    own_a = pltpu.make_async_copy(a_ref, ag_ref.at[v, pl.ds(0, cap_a)], own_sem.at[1])
+    own_a.start()
+    for step in range(1, n - 1):
+        for piece in order:
+            b_copies[step - 1, piece].wait_recv()
+            b_copies[step, piece] = b_copy(step, piece)
+            b_copies[step, piece].start()
+    to_across.wait_recv()
+    forward = a_copy(2, ag_ref.at[across, pl.ds(0, cap_a)], across, mate)
+    forward.start()
+    for piece in order:
+        b_copies[n - 2, piece].wait_recv()
+    to_mate.wait_recv()
+    forward.wait_recv()
+    for step in range(n - 1):
+        for piece in order:
+            b_copies[step, piece].wait_send()
+    to_across.wait_send()
+    to_mate.wait_send()
+    forward.wait_send()
+    own_b.wait()
+    own_a.wait()
+
+
+def exchange(n, which, cap_a, cap_b, amplitudes, integrals, a_index, b_index):
+    packed_a = pack(a_index, amplitudes, cap_a)
+    packed_b = pack(b_index, integrals, cap_b)
+    any_spec = pl.BlockSpec(memory_space=pl.ANY)
+    return pl.pallas_call(
+        functools.partial(exchange_kernel, n, cap_a, cap_b),
+        out_shape=(
+            jax.ShapeDtypeStruct((4, 4, SQUARE, SQUARE), amplitudes.dtype),
+            jax.ShapeDtypeStruct((n, 2, SQUARE, SQUARE), integrals.dtype),
+        ),
+        in_specs=[any_spec, any_spec],
+        out_specs=(any_spec, any_spec),
+        scratch_shapes=[
+            pltpu.SemaphoreType.DMA((2,)),
+            pltpu.SemaphoreType.DMA((3,)),
+            pltpu.SemaphoreType.DMA((3,)),
+            pltpu.SemaphoreType.DMA((n - 1, PIECES)),
+            pltpu.SemaphoreType.DMA((n - 1, PIECES)),
+        ],
+        compiler_params=pltpu.CompilerParams(collective_id=which, has_side_effects=True),
+        name="exchange",
+    )(packed_a, packed_b)
+
+
+def ladder_kernel(
+    count_ref, keep_ref, a_slot, b_slot, a_ref, b_ref, other_ref, occ_ref, vir_ref, out_ref, acc
+):
+    block = pl.program_id(0)
+    step = pl.program_id(1)
+    count = count_ref[block]
+    a_block = a_ref.at[0]
+    b_block = b_ref.at[0]
+
+    @pl.when(step == 0)
+    def _():
+        acc[...] = jnp.zeros_like(acc)
+
+    @pl.when(step < count)
+    def _():
+        @pl.loop(0, SQUARE // STEP_COLS)
+        def _(part):
+            cols = pl.ds(pl.multiple_of(part * STEP_COLS, STEP_COLS), STEP_COLS)
+            acc[:, cols] += jnp.dot(
+                a_block[...], b_block[:, cols], preferred_element_type=jnp.float32
+            )
+
+    last = step == pl.num_programs(1) - 1
+
+    @pl.when(last & (keep_ref[block] == 1))
+    def _():
+        @pl.loop(0, SQUARE // 128)
+        def _(part):
+            cut = pl.ds(pl.multiple_of(part * 128, 128), 128)
+            denom = occ_ref[0, cut, :] - vir_ref[0]
+            total = acc[cut, :] + other_ref[cut, :].astype(jnp.float32)
+            out_ref[cut, :] = (total / denom).astype(out_ref.dtype)
+
+    @pl.when(last & (keep_ref[block] == 0))
+    def _():
+        out_ref[...] = jnp.zeros_like(out_ref)
+
+
+def ladder(count, keep, a_slot, b_slot, steps, a_all, b_all, other_terms, occ_sum, vir_sum):
+    square = (SQUARE, SQUARE)
+    return pl.pallas_call(
+        ladder_kernel,
+        out_shape=jax.ShapeDtypeStruct(other_terms.shape, other_terms.dtype),
+        grid_spec=pltpu.PrefetchScalarGridSpec(
+            num_scalar_prefetch=4,
+            grid=(4, steps),
+            in_specs=[
+                pl.BlockSpec((1,) + square, lambda b, j, c, k, sa, sb: (sa[b * steps + j], 0, 0)),
+                pl.BlockSpec((1,) + square, lambda b, j, c, k, sa, sb: (sb[b * steps + j], 0, 0)),
+                pl.BlockSpec(square, lambda b, j, c, k, sa, sb: (b // 2, b % 2)),
+                pl.BlockSpec((1, SQUARE, 1), lambda b, j, c, k, sa, sb: (b // 2, 0, 0)),
+                pl.BlockSpec((1, 1, SQUARE), lambda b, j, c, k, sa, sb: (b % 2, 0, 0)),
+            ],
+            out_specs=pl.BlockSpec(square, lambda b, j, c, k, sa, sb: (b // 2, b % 2)),
+            scratch_shapes=[pltpu.VMEM(square, jnp.float32)],
+        ),
+        compiler_params=pltpu.CompilerParams(vmem_limit_bytes=48 << 20),
+        name="ladder",
+    )(count, keep, a_slot, b_slot, a_all, b_all, other_terms, occ_sum, vir_sum)
+
+
+def ranks(flags):
+    size = flags.shape[-1]
+    before = jnp.arange(size)[:, None] < jnp.arange(size)[None, :]
+    return jnp.sum(jnp.where(before, flags[..., :, None], 0), axis=-2)
+
+
+def pick(flags, rank, values, size):
+    total = jnp.sum(flags, axis=-1, keepdims=True)
+    want = jnp.minimum(jnp.arange(size), jnp.maximum(total - 1, 0))
+    hit = (flags[..., :, None] == 1) & (rank[..., :, None] == want[..., None, :])
+    return jnp.sum(jnp.where(hit, values[..., :, None], 0), axis=-2)
+
+
+def block_device(
+    amplitudes,
+    integrals,
+    other_terms,
+    occ_irrep,
+    vir_irrep,
+    pair_tiles,
+    spin_mask,
+    occ_energy,
+    vir_energy,
+):
+    o = lax.axis_index("occ")
+    v = lax.axis_index("vir")
+    allowed, _ = symmetry(occ_irrep, vir_irrep, pair_tiles, spin_mask)
+    allowed = allowed.astype(jnp.int32)
+    pairs = allowed.shape[1]
+    occ_devices = allowed.shape[0] // 2
+    used = jnp.max(allowed[:, :, None] * allowed[:, None, :], axis=0)
+    a_flags = allowed.reshape(occ_devices, 2, 4, 2).transpose(0, 2, 1, 3).reshape(occ_devices, 4, 4)
+    b_flags = used.reshape(pairs, 4, 2)
+    a_most = jnp.max(jnp.sum(a_flags, axis=-1))
+    b_most = jnp.max(jnp.sum(b_flags, axis=-1))
+
+    a_here = lax.dynamic_index_in_dim(a_flags, o, 0, keepdims=False)
+    a_rank = ranks(a_here)
+    b_here = lax.dynamic_index_in_dim(b_flags, v, 1, keepdims=False)
+    b_rank = ranks(b_here)
+    a_mine = lax.dynamic_index_in_dim(a_here, v, 0, keepdims=False)
+    b_mine = lax.dynamic_index_in_dim(b_here, o, 0, keepdims=False)
+    a_index = pick(a_mine, ranks(a_mine), jnp.arange(4, dtype=jnp.int32), 4)
+    b_index = pick(b_mine, ranks(b_mine), jnp.arange(2, dtype=jnp.int32), 2)
+
+    variant = jnp.where(b_most > 1, 2, jnp.where(a_most > 2, 1, 0))
+    run = functools.partial(exchange, occ_devices)
+    a_all, b_all = lax.switch(
+        variant,
+        [
+            functools.partial(run, 0, 2, 1),
+            functools.partial(run, 1, 4, 1),
+            functools.partial(run, 2, 4, 2),
+        ],
+        amplitudes,
+        integrals,
+        a_index,
+        b_index,
+    )
+
+    a_rows = a_here.reshape(4, 2, 2).transpose(1, 0, 2).reshape(2, pairs)
+    a_at = (a_rank + 4 * jnp.arange(4, dtype=jnp.int32)[:, None]).reshape(4, 2, 2)
+    a_at = a_at.transpose(1, 0, 2).reshape(2, pairs)
+    b_at = (b_rank + 2 * jnp.arange(pairs, dtype=jnp.int32)[:, None]).T
+    keep = a_mine.reshape(2, 2)
+    terms = a_rows[:, None, :] * keep[:, :, None]
+    order = ranks(terms)
+    a_slot = pick(terms, order, jnp.broadcast_to(a_at[:, None, :], terms.shape), pairs)
+    b_slot = pick(terms, order, jnp.broadcast_to(b_at[None, :, :], terms.shape), pairs)
+    count = jnp.sum(terms, axis=-1).reshape(-1)
+
+    occ_tiles = occ_energy.reshape(OTILES, TILE)
+    pair_occ = (occ_tiles[:, None, :, None] + occ_tiles[None, :, None, :]).reshape(-1, SQUARE)
+    occ_sum = lax.dynamic_slice_in_dim(pair_occ, 2 * o, 2, 0)[:, :, None]
+    vir_tiles = vir_energy.reshape(-1, TILE)
+    tiles = lax.dynamic_slice_in_dim(pair_tiles, 2 * v, 2, 0)
+    first = lookup(tiles[:, 0], vir_tiles)
+    second = lookup(tiles[:, 1], vir_tiles)
+    vir_sum = (first[:, :, None] + second[:, None, :]).reshape(2, 1, SQUARE)
+
+    return ladder(
+        count,
+        keep.reshape(-1),
+        a_slot.reshape(-1),
+        b_slot.reshape(-1),
+        pairs,
+        a_all.reshape(-1, SQUARE, SQUARE),
+        b_all.reshape(-1, SQUARE, SQUARE),
+        other_terms,
+        occ_sum,
+        vir_sum,
+    )
+
+
+def per_device(amplitudes, integrals, *rest):
+    blocks = amplitudes.shape == (2 * SQUARE, 2 * SQUARE)
+    blocks = blocks and integrals.shape == (SQUARE, 2 * SQUARE) and lax.axis_size("vir") == 4
+    blocks = blocks and lax.axis_size("occ") == OTILES * OTILES // 2
+    device = block_device if blocks else dense_device
+    return device(amplitudes, integrals, *rest)
+
+
 def solution(mesh):
     in_specs = (P("occ", "vir"), P("occ", "vir"), P("occ", "vir"), P(), P(), P(), P(), P(), P())
     out_specs = P("occ", "vir")

time: 1030 us -> 243 us (0.24)
  waiting for transfers between devices: 798 us -> 0 us
  Pallas kernels: 0 us -> 229 us
  other arithmetic: 107 us -> 8.1 us
  matrix products: 85.7 us -> 0 us
  local copies, waits for them, and re-layouts: 24.9 us -> 3.6 us
  between operations: 13.5 us -> 1.46 us
    all_gather x2 -> x0, waiting for transfers between devices: 798 us -> none  [the longest x1 638 us: per_device(): lax.all_gather(masked_slab, 'occ', axis=0, tiled=True)]
    pallas_call x0 -> x4, Pallas kernels: none -> 229 us  [the longest x1 194 us: exchange(): pl.pallas_call(functools.partial(exchange_kernel, n, cap_a, cap_b), out_s...]
    dot_general x1 -> x0, matrix products: 85.7 us -> none  [add_block(): return jnp.dot(amp_cols, slab_rows, preferred_element_type=jnp.float32)]
    reduce_sum x8 -> x2, other arithmetic: 85 us -> 0.96 us  [lookup(): jnp.sum(jnp.where(hits[:, :, None], table[None, :, :], jnp.zeros_like(tab...]
    select_n x7 -> x0, other arithmetic: 20.7 us -> none  [the longest x1 12.2 us: per_device(): jnp.where(amp_keep > 0.5, amplitudes, jnp.zeros_like(amplitudes))]
    reduce_sum x1, local copies, waits for them, and re-layouts: 17.6 us -> 0.1 us  [ranks(): return jnp.sum(jnp.where(before, flags[..., :, None], 0), axis=-2)]
  transfers between devices with their start and end apart: 2 -> 0, of which waited for: 2 -> 0; matrix products, arithmetic and copies ran while one was open for 4% -> 0% of each run, Pallas kernels for 0% -> 0%
where the time goes in v1:
time: 243 us
  Pallas kernels  229 us (94%)
  other arithmetic  8.1 us (3%)
  local copies, waits for them, and re-layouts  3.6 us (1%)
    pallas_call x1, Pallas kernels, exchange(): pl.pallas_call(functools.partial(exchange_kernel, n, cap_a, cap_b), out_s...  194 us
    pallas_call x1, Pallas kernels, ladder(): pl.pallas_call(ladder_kernel, out_shape=jax.ShapeDtypeStruct(other_terms....  26.2 us
    pallas_call x2, Pallas kernels, pack(): pl.pallas_call(pack_kernel, out_shape=jax.ShapeDtypeStruct((slots, SQUARE...  8.74 us

profile of v1, /device:TPU:20, one launch (start us, length us, event | category | flops | bytes accessed | tf_op | source)
XLA Modules:
  0.0 243.3 jit_solution(10741863066588809371)
XLA Ops:
  0.0 0.8 broadcast_xor_fusion
  0.9 0.8 slice_bitcast_fusion.3
  1.6 0.9 select_reduce_fusion.15
  2.5 0.8 select_convert_fusion
  3.4 0.1 copy.51
  3.5 0.2 fusion.12
  3.8 0.2 fusion.11
  4.0 0.1 copy.52
  4.1 0.1 copy.53
  4.3 0.2 broadcast_multiply_fusion
  4.6 0.2 multiply_reduce_fusion
  5.3 0.1 copy.54
  5.4 0.1 copy.55
  5.6 0.1 select_reduce_fusion.11
  5.9 0.6 reduce_max.28
  7.2 0.1 bitcast_reduce_fusion
  7.4 0.6 reduce_max.29
  8.8 207.1 %conditional.1 = (bf16[16,1024,1024]{2,1,0:T(8,128)(2,1)}, bf16[16,1024,1024]{2,1,0:T(8,128)(2,1)}) conditional(s32[]{:T(128)} %clamp.15, (s32[1,1,4]{0,2,1:T(4,128)S(1)}, s32[4]{0:T(128)S(1)}, pred[4,4]{1,0:T(4,128)(4,1)S(1)}, s32[4,4]{1,0:T(4,128)S(1)}, s32[1,4]{1,0:T(1,128)S(1)}, /*index=5*/s32[4,4]{1,0:T(4,128)S(1)}, ...), branch_computations={%region_13.20_spmd, %region_20.27_spmd, %region_27.34_spmd} | conditional | flops 128 | bytes 600 | solution.py:324
  8.8 0.6 reduce_sum.222
  10.2 0.1 copy.70
  10.3 0.7 select_reduce_fusion.index_ref
  11.0 5.4 %pack.6.a_ref = bf16[2,1024,1024]{2,1,0:T(8,128)(2,1)} custom-call(s32[4]{0:T(128)} %select_reduce_fusion.index_ref, bf16[2048,2048]{1,0:T(8,128)(2,1)} %get-tuple-element.436.block_ref), custom_call_target="tpu_custom_call" | custom-call | tf_op jit(solution)/shard_map/cond/branch_0_fun/pack/pallas_call | solution.py:91
  16.5 0.1 copy.58
  16.6 0.7 reduce_sum.228
  18.1 0.7 fusion.index_ref
  18.7 3.3 %pack.7.b_ref = bf16[1,1024,1024]{2,1,0:T(8,128)(2,1)} custom-call(s32[2]{0:T(128)} %fusion.index_ref, bf16[1024,2048]{1,0:T(8,128)(2,1)} %get-tuple-element.442.block_ref), custom_call_target="tpu_custom_call" | custom-call | tf_op jit(solution)/shard_map/cond/branch_0_fun/pack/pallas_call | solution.py:91
  22.0 193.8 %exchange.6 = (bf16[4,4,1024,1024]{3,2,1,0:T(8,128)(2,1)}, bf16[8,2,1024,1024]{3,2,1,0:T(8,128)(2,1)}) custom-call(bf16[2,1024,1024]{2,1,0:T(8,128)(2,1)} %pack.6.a_ref, bf16[1,1024,1024]{2,1,0:T(8,128)(2,1)} %pack.7.b_ref), custom_call_target="tpu_custom_call" | custom-call | tf_op jit(solution)/shard_map/cond/branch_0_fun/exchange/pallas_call | solution.py:196
  216.1 0.1 add.118
  216.2 0.4 copy.63.occ_ref
  216.9 0.1 select_reduce_fusion.10
  216.9 0.1 fusion.4
  217.1 26.2 %ladder.1 = bf16[2048,2048]{1,0:T(8,128)(2,1)} custom-call(s32[4]{0:T(128)S(1)} %reshape.368.count_ref, s32[4]{0:T(128)S(1)} %get-tuple-element.641.keep_ref, s32[32]{0:T(128)S(1)} %reshape.369.a_slot, s32[32]{0:T(128)S(1)} %reshape.371.b_slot, bf16[16,1024,1024]{2,1,0:T(8,128)(2,1)} %get-tuple-element.477.a_ref, ...), custom_call_target="tpu_custom_call" | custom-call | tf_op jit(solution)/shard_map/ladder/pallas_call | solution.py:256
  (52 shorter events, 2.0 us)
Async XLA Ops:
  8.8 207.1 %copy-start.2 = (f32[128]{0:T(128)S(1)}, f32[128]{0:T(128)}, u32[]{:S(2)}) copy-start(f32[128]{0:T(128)} %param.19) | copy-start | bytes 1540
  8.8 207.8 %copy-start = (f32[1024]{0:T(1024)S(1)}, f32[1024]{0:T(1024)}, u32[]{:S(2)}) copy-start(f32[1024]{0:T(1024)} %param.20) | copy-start | bytes 12292
  8.8 207.9 %copy-start.1 = (s32[8,2]{0,1:T(2,128)S(1)}, s32[8,2]{0,1:T(2,128)}, u32[]{:S(2)}) copy-start(s32[8,2]{0,1:T(2,128)} %param.17) | copy-start | bytes 196
